TPU v7x, 32 devices: a whole 2x2x4 slice. The times are simulated.
32 devices in a mesh: clips: 2 (over y), row: 4 (over x, core), col: 4 (over z).
Axes of the slice: x: 2, y: 2, z: 4, core: 2. Of those that a mesh axis runs over, the one named last changes fastest.
Arguments:
- clip_tokens: bfloat16 [2048, 6144], P(('clips', 'col'), 'row'), parts along dimension 0, may hold values from -12 to 12
- modulation: float32 [8, 6, 6144], P('clips', None, 'row'), parts along dimension 0, may hold values from -3 to 3
- w_qkv: bfloat16 [6144, 3, 4096], P('row', None, 'col'), may hold values from -3 to 3
- w_out: bfloat16 [4096, 6144], P('col', 'row'), may hold values from -0.09375 to 0.09375
- w_up: bfloat16 [6144, 12288], P('row', 'col'), may hold values from -0.078125 to 0.078125
- up_bias: float32 [12288], P('col'), may hold values from -3 to 3
- w_down: bfloat16 [12288, 6144], P('col', 'row'), may hold values from -0.0546875 to 0.0546875
- guide_num: int32 [8], P('clips'), parts along dimension 0, may hold values from -3 to 10, as said below
Outputs:
- guided: bfloat16 [512, 6144], P(('clips', 'col'), 'row'), parts along dimension 0
There are 2 independent parts, one for each index of `clips`. A program takes and returns all parts, laid end to end along the dimension named above; an argument that names none is the same for every part. Nothing has to cross between parts.
Inputs may be any that keep to these rules, and one draw needn't show every extreme that they name: `guide_num`: the three negative numerators are -1, -2 and -3 in some order, and the positive one makes the four sum to 4.
All inputs are finite; a program needn't handle non-finite values.
Results may differ from a plain program's by a relative error of at most 0.019.
Values may be sent and summed in bfloat16 or wider, within the bound.
A program may use at most 128 MiB of HBM per device.

v0:
```python
import jax
import jax.numpy as jnp
from jax import lax
from jax.sharding import PartitionSpec as P

D = 6144
HEAD_DIM = 128
eps = 1e-06


def normalize(values, shift, scale):
    totals = lax.psum((jnp.sum(values, axis=1), jnp.sum(values * values, axis=1)), "row")
    mean = totals[0] / D
    variance = totals[1] / D - mean * mean
    normed = (values - mean[:, None]) * lax.rsqrt(variance + eps)[:, None]
    branches = shift.shape[0]
    shaped = normed.reshape(-1, branches, values.shape[1]) * (1.0 + scale[None]) + shift[None]
    return shaped.reshape(values.shape)


def general_layer(clip_tokens, modulation, w_qkv, w_out, w_up, up_bias, w_down, guide_num):
    branches = modulation.shape[0]
    feat_rows = w_qkv.shape[0]
    head_cols = w_qkv.shape[2]
    heads_here = head_cols // HEAD_DIM
    x_rows = clip_tokens.astype(jnp.float32)
    first = normalize(x_rows, modulation[:, 0], modulation[:, 1]).astype(jnp.bfloat16)
    w_flat = w_qkv.reshape(feat_rows, 3 * head_cols)
    partial_qkv = jnp.dot(
        lax.all_gather(first, "col", axis=0, tiled=True), w_flat, preferred_element_type=jnp.float32
    )
    scale_score = 1.0 / jnp.sqrt(jnp.float32(HEAD_DIM))
    qkv = lax.psum_scatter(partial_qkv.astype(jnp.bfloat16), "row", scatter_dimension=0, tiled=True)
    query3 = qkv[:, :head_cols].reshape(-1, heads_here, HEAD_DIM)
    query_rows = query3.shape[0]
    piece = (
        lax.all_gather(qkv[:, head_cols : 2 * head_cols], "row", axis=0, tiled=True),
        lax.all_gather(qkv[:, 2 * head_cols :], "row", axis=0, tiled=True),
    )
    top = jnp.full((heads_here, query_rows), -1e30, jnp.float32)
    rows = piece[0].shape[0]
    key_heads = piece[0].reshape(rows, heads_here, HEAD_DIM)
    value_heads = piece[1].reshape(rows, heads_here, HEAD_DIM)
    scores = (
        jnp.einsum("qhd,khd->hqk", query3, key_heads, preferred_element_type=jnp.float32)
        * scale_score
    )
    query_branch = jnp.arange(query3.shape[0], dtype=jnp.int32) % branches
    key_branch = jnp.arange(rows, dtype=jnp.int32) % branches
    allowed = (query_branch[:, None] == key_branch[None, :])[None]
    masked = jnp.where(allowed, scores, -1e30)
    new_top = jnp.maximum(top, jnp.max(masked, axis=-1))
    weights = jnp.where(allowed, jnp.exp(masked - new_top[..., None]), 0.0)
    denom = jnp.sum(weights, axis=-1)
    accum = jnp.einsum(
        "hqk,khd->hqd",
        weights.astype(jnp.bfloat16),
        value_heads,
        preferred_element_type=jnp.float32,
    )
    att = (accum / denom[..., None]).transpose(1, 0, 2).reshape(-1, head_cols).astype(jnp.bfloat16)
    partial_out = jnp.dot(
        lax.all_gather(att, "row", axis=0, tiled=True), w_out, preferred_element_type=jnp.float32
    )
    out_rows = lax.psum_scatter(
        partial_out.astype(jnp.bfloat16), "col", scatter_dimension=0, tiled=True
    ).astype(jnp.float32)
    by_branch = x_rows.shape[0] // branches
    resid = (
        x_rows.reshape(by_branch, branches, feat_rows)
        + modulation[None, :, 2] * out_rows.reshape(by_branch, branches, feat_rows)
    ).reshape(x_rows.shape)
    second = normalize(resid, modulation[:, 3], modulation[:, 4]).astype(jnp.bfloat16)
    partial_up = jnp.dot(
        lax.all_gather(second, "col", axis=0, tiled=True), w_up, preferred_element_type=jnp.float32
    )
    up_rows = lax.psum_scatter(
        partial_up.astype(jnp.bfloat16), "row", scatter_dimension=0, tiled=True
    ).astype(jnp.float32)
    act = jax.nn.gelu(up_rows + up_bias[None], approximate=True).astype(jnp.bfloat16)
    partial_down = jnp.dot(
        lax.all_gather(act, "row", axis=0, tiled=True), w_down, preferred_element_type=jnp.float32
    )
    guide_weights = guide_num.astype(jnp.float32) / 4.0
    weights_gate = guide_weights[:, None] * modulation[:, 5]
    combined = jnp.sum(partial_down.reshape(-1, branches, feat_rows) * weights_gate[None], axis=1)
    mlp_rows = lax.psum_scatter(
        combined.astype(jnp.bfloat16), "col", scatter_dimension=0, tiled=True
    ).astype(jnp.float32)
    resid_mix = jnp.sum(
        resid.reshape(by_branch, branches, feat_rows) * guide_weights[None, :, None], axis=1
    )
    return (resid_mix + mlp_rows).astype(jnp.bfloat16)


BF = jnp.bfloat16


def swap_row(value, distance):
    size = lax.axis_size("row")
    return lax.ppermute(value, "row", [(r, r ^ distance) for r in range(size)])


def sum_over_row(value):
    value = value + swap_row(value, 1)
    return value + swap_row(value, 2)


def scatter_row(pieces):
    me = lax.axis_index("row")
    half, core = (me // 2, me % 2)
    mine = lax.dynamic_index_in_dim(pieces, core, 1, keepdims=False)
    theirs = lax.dynamic_index_in_dim(pieces, 1 - core, 1, keepdims=False)
    got = swap_row(theirs, 1)
    away = lax.dynamic_index_in_dim(mine, 1 - half, 0, keepdims=False).astype(
        jnp.float32
    ) + lax.dynamic_index_in_dim(got, 1 - half, 0, keepdims=False).astype(jnp.float32)
    came = swap_row(away.astype(BF), 2)
    kept = lax.dynamic_index_in_dim(mine, half, 0, keepdims=False).astype(
        jnp.float32
    ) + lax.dynamic_index_in_dim(got, half, 0, keepdims=False).astype(jnp.float32)
    return kept + came.astype(jnp.float32)


def gather_row(value):
    me = lax.axis_index("row")
    half, core = (me // 2, me % 2)
    other = swap_row(value, 2)
    pair = jnp.where(half == 0, jnp.stack([value, other]), jnp.stack([other, value]))
    beside = swap_row(pair, 1)
    return jnp.where(
        core == 0, jnp.stack([pair, beside], axis=1), jnp.stack([beside, pair], axis=1)
    )


def moments(values):
    return jnp.stack([jnp.sum(values, axis=1), jnp.sum(values * values, axis=1)])


def apply_norm(values, totals, shift, scale):
    mean = totals[0] / D
    variance = totals[1] / D - mean * mean
    normed = (values - mean[:, None]) * lax.rsqrt(variance + eps)[:, None]
    return (normed * (1.0 + scale[None]) + shift[None]).astype(BF)


def attend(q, k, v):
    scores = jnp.einsum("qhd,khd->hqk", q, k, preferred_element_type=jnp.float32)
    scores = scores / jnp.sqrt(jnp.float32(HEAD_DIM))
    weights = jnp.exp(scores - jnp.max(scores, axis=-1, keepdims=True))
    denom = jnp.sum(weights, axis=-1)
    mixed = jnp.einsum("hqk,khd->hqd", weights.astype(BF), v, preferred_element_type=jnp.float32)
    mixed = mixed / denom[..., None]
    return mixed.transpose(1, 0, 2).reshape(q.shape[0], -1).astype(BF)


def branch_layer(clip_tokens, modulation, w_qkv, w_out, w_up, up_bias, w_down, guide_num):
    branches = modulation.shape[0]
    feat_rows, _, head_cols = w_qkv.shape
    here = clip_tokens.shape[0] // branches
    w_flat = w_qkv.reshape(feat_rows, 3 * head_cols)
    by_branch = clip_tokens.reshape(here, branches, feat_rows).transpose(1, 0, 2)
    mine = head_cols // 4
    guide = guide_num.astype(jnp.float32) / 4.0
    total = None
    mixed = None
    for b in range(branches):
        x = by_branch[b]
        x_all = lax.all_gather(x, "col", axis=0, tiled=True).astype(jnp.float32)
        tokens = x_all.shape[0]
        first = apply_norm(x_all, sum_over_row(moments(x_all)), modulation[b, 0], modulation[b, 1])
        partial = jnp.dot(first, w_flat, preferred_element_type=jnp.float32).astype(BF)
        pieces = partial.reshape(tokens, 3, 2, 2, mine).transpose(2, 3, 1, 0, 4)
        qkv = scatter_row(pieces).astype(BF).reshape(3, tokens, mine // HEAD_DIM, HEAD_DIM)
        att = attend(qkv[0], qkv[1], qkv[2])
        att_all = gather_row(att).reshape(4, tokens, mine).transpose(1, 0, 2).reshape(tokens, -1)
        partial = jnp.dot(att_all, w_out, preferred_element_type=jnp.float32).astype(BF)
        out = lax.psum_scatter(partial, "col", scatter_dimension=0, tiled=True)
        resid = x.astype(jnp.float32) + modulation[b, 2][None] * out.astype(jnp.float32)
        second = apply_norm(resid, sum_over_row(moments(resid)), modulation[b, 3], modulation[b, 4])
        second_all = lax.all_gather(second, "col", axis=0, tiled=True)
        partial = jnp.dot(second_all, w_up, preferred_element_type=jnp.float32).astype(BF)
        up = scatter_row(partial.reshape(2, 2, tokens // 4, -1))
        act = jax.nn.gelu(up + up_bias[None], approximate=True).astype(BF)
        act_all = gather_row(act).reshape(tokens, -1)
        down = jnp.dot(act_all, w_down, preferred_element_type=jnp.float32)
        down = down * (guide[b] * modulation[b, 5])[None]
        total = down if total is None else total + down
        part = guide[b] * resid
        mixed = part if mixed is None else mixed + part
    mlp = lax.psum_scatter(total.astype(BF), "col", scatter_dimension=0, tiled=True)
    return (mixed + mlp.astype(jnp.float32)).astype(BF)


def on_device(*args):
    heads_here = args[2].shape[2] // HEAD_DIM
    if lax.axis_size("row") == 4 and heads_here % 4 == 0:
        return branch_layer(*args)
    return general_layer(*args)


def solution(mesh):
    in_specs = (
        P(("clips", "col"), "row"),
        P("clips", None, "row"),
        P("row", None, "col"),
        P("col", "row"),
        P("row", "col"),
        P("col"),
        P("col", "row"),
        P("clips"),
    )
    out_specs = P(("clips", "col"), "row")
    return jax.shard_map(
        on_device, mesh=mesh, in_specs=in_specs, out_specs=out_specs, check_vma=False
    )
```

profile of v0, /device:TPU:0, one launch (start us, length us, event | category | flops | bytes accessed | tf_op | source)
XLA Modules:
  0.0 575.6 jit_solution(8317175544174087421)
XLA Ops:
  10.4 21.3 %all-gather.3 = bf16[1,256,1536]{2,1,0:T(8,128)(2,1)S(1)} all-gather(bf16[1,64,1536]{2,1,0:T(8,128)(2,1)S(1)} %get-tuple-element.56), channel_id=5, replica_groups=mesh['clips'=2,'row'=4,'col'=4] {'col'}, dimensions={1}, use_global_device_ids=true | all-gather | bytes 983040 | tf_op jit(solution)/shard_map/all_gather | solution.py:169
  32.2 18.0 %all-gather.2 = bf16[1,256,1536]{2,1,0:T(8,128)(2,1)S(1)} all-gather(bf16[1,64,1536]{2,1,0:T(8,128)(2,1)S(1)} %get-tuple-element.55), channel_id=4, replica_groups=mesh['clips'=2,'row'=4,'col'=4] {'col'}, dimensions={1}, use_global_device_ids=true | all-gather | bytes 983040 | tf_op jit(solution)/shard_map/all_gather | solution.py:169
  51.1 18.1 %all-gather.1 = bf16[1,256,1536]{2,1,0:T(8,128)(2,1)S(1)} all-gather(bf16[1,64,1536]{2,1,0:T(8,128)(2,1)S(1)} %get-tuple-element.57), channel_id=3, replica_groups=mesh['clips'=2,'row'=4,'col'=4] {'col'}, dimensions={1}, use_global_device_ids=true | all-gather | bytes 983040 | tf_op jit(solution)/shard_map/all_gather | solution.py:169
  70.2 18.7 %all-gather = bf16[1,256,1536]{2,1,0:T(8,128)(2,1)S(1)} all-gather(bf16[1,64,1536]{2,1,0:T(8,128)(2,1)S(1)} %get-tuple-element.58), channel_id=2, replica_groups=mesh['clips'=2,'row'=4,'col'=4] {'col'}, dimensions={1}, use_global_device_ids=true | all-gather | bytes 983040 | tf_op jit(solution)/shard_map/all_gather | solution.py:169
  92.2 2.7 multiply_reduce_fusion.7
  94.9 12.7 %copy.38 = bf16[1536,3,1024]{0,2,1:T(8,128)(2,1)} copy(bf16[1536,3,1024]{2,0,1:T(8,128)(2,1)} %param.10) | data formatting | bytes 18874368 | tf_op args[2]
  112.0 7.8 %convolution_convert_fusion.4 = bf16[256,3072]{1,0:T(8,128)(2,1)} fusion(bf16[1536,3072]{0,1:T(8,128)(2,1)} %bitcast.477, bf16[1,256,1536]{2,1,0:T(8,128)(2,1)} %copy-done.14, f32[1536]{0:T(1024)S(1)} %get-tuple-element.29, f32[1536]{0:T(1024)S(1)} %get-tuple-element.30, f32[256]{0:T(256)S(1)} %add_rsqrt_fusion, f32[256]{0:T(256)S(1)} %bitcast.609), kind=kOutput, calls=%fused_computation.4 | convolution fusion | flops 2419064832 | bytes 11810816 | tf_op jit(solution)/shard_map/dot_general | solution.py:172
  119.8 5.0 reshape.1011
  124.8 3.0 constant_dynamic-slice_fusion.1
  129.2 11.0 %convolution_convert_fusion.5 = bf16[256,3072]{1,0:T(8,128)(2,1)} fusion(bf16[1536,3072]{0,1:T(8,128)(2,1)} %bitcast.478, bf16[1,256,1536]{2,1,0:T(8,128)(2,1)S(1)} %copy-done.13, f32[1536]{0:T(1024)S(1)} %get-tuple-element.32, f32[1536]{0:T(1024)S(1)} %get-tuple-element.33, f32[256]{0:T(256)S(1)} %add_rsqrt_fusion.1, f32[256]{0:T(256)S(1)} %bitcast.611), kind=kOutput, calls=%fused_computation.5 | convolution fusion | flops 2419064832 | bytes 11810816 | tf_op jit(solution)/shard_map/dot_general | solution.py:172
  140.2 5.2 reshape.1009
  145.4 3.0 constant_dynamic-slice_fusion.4
  149.8 11.0 %convolution_convert_fusion.6 = bf16[256,3072]{1,0:T(8,128)(2,1)} fusion(bf16[1536,3072]{0,1:T(8,128)(2,1)} %bitcast.479, bf16[1,256,1536]{2,1,0:T(8,128)(2,1)S(1)} %copy-done.11, f32[1536]{0:T(1024)S(1)} %get-tuple-element.36, f32[1536]{0:T(1024)S(1)} %get-tuple-element.37, f32[256]{0:T(256)S(1)} %add_rsqrt_fusion.2, f32[256]{0:T(256)S(1)} %bitcast.613), kind=kOutput, calls=%fused_computation.6 | convolution fusion | flops 2419064832 | bytes 11810816 | tf_op jit(solution)/shard_map/dot_general | solution.py:172
  160.8 5.0 reshape.1007
  165.8 3.0 constant_dynamic-slice_fusion.7
  170.2 11.0 %convolution_convert_fusion.7 = bf16[256,3072]{1,0:T(8,128)(2,1)} fusion(bf16[1536,3072]{0,1:T(8,128)(2,1)} %bitcast.480, bf16[1,256,1536]{2,1,0:T(8,128)(2,1)S(1)} %copy-done.9, f32[1536]{0:T(1024)S(1)} %get-tuple-element.39, f32[1536]{0:T(1024)S(1)} %get-tuple-element.40, f32[256]{0:T(256)S(1)} %add_rsqrt_fusion.3, f32[256]{0:T(256)S(1)} %bitcast.607), kind=kOutput, calls=%fused_computation.7 | convolution fusion | flops 2419064832 | bytes 11810816 | tf_op jit(solution)/shard_map/dot_general | solution.py:172
  181.2 5.4 reshape.1005
  186.6 3.0 constant_dynamic-slice_fusion.10
  210.1 3.2 collective-permute-done.21
  226.7 14.1 %collective-permute-done.22 = bf16[256,256]{1,0:T(8,128)(2,1)S(1)} collective-permute-done((bf16[256,256]{1,0:T(8,128)(2,1)}, bf16[256,256]{1,0:T(8,128)(2,1)S(1)}, u32[]{:S(2)}, u32[]{:S(2)}) %collective-permute-start.22) | collective-permute-done | bytes 131104 | tf_op jit(solution)/shard_map/ppermute | solution.py:101
  249.6 3.1 convolution_convert_fusion.8
  272.7 3.0 convolution_convert_fusion.9
  296.7 3.0 convolution_convert_fusion.10
  303.1 4.5 collective-permute-done.4
  314.2 3.0 convolution_convert_fusion.11
  317.3 8.5 %reduce-scatter.8.cloned.1.call-done = bf16[64,1536]{1,0:T(8,128)(2,1)} async-done(((bf16[256,1536]{1,0:T(8,128)(2,1)}), bf16[64,1536]{1,0:T(8,128)(2,1)}) %reduce-scatter.8.cloned.1.call-update) | async-done | bytes 196624 | tf_op jit(solution)/shard_map/reduce_scatter | solution.py:178
  325.9 24.8 %reduce-scatter.6.cloned.1.call-done = bf16[64,1536]{1,0:T(8,128)(2,1)} async-done(((bf16[256,1536]{1,0:T(8,128)(2,1)}), bf16[64,1536]{1,0:T(8,128)(2,1)}) %reduce-scatter.6.cloned.1.call-update) | async-done | bytes 196624 | tf_op jit(solution)/shard_map/reduce_scatter | solution.py:178
  361.7 18.1 %all_gather.31 = bf16[256,1536]{1,0:T(8,128)(2,1)S(1)} all-gather(bf16[64,1536]{1,0:T(8,128)(2,1)S(1)} %get-tuple-element.54), channel_id=1, replica_groups=mesh['clips'=2,'row'=4,'col'=4] {'col'}, dimensions={0}, use_global_device_ids=true | all-gather | bytes 983040 | tf_op jit(solution)/shard_map/all_gather | solution.py:181
  379.8 6.4 %convolution_convert_fusion = bf16[256,3072]{1,0:T(8,128)(2,1)S(1)} fusion(bf16[256,1536]{1,0:T(8,128)(2,1)S(1)} %all_gather.31, bf16[1536,3072]{1,0:T(8,128)(2,1)} %param.12), kind=kOutput, calls=%fused_computation | convolution fusion | flops 2416705536 | bytes 11796480 | tf_op jit(solution)/shard_map/dot_general | solution.py:182
  387.6 18.0 %all_gather.30 = bf16[256,1536]{1,0:T(8,128)(2,1)S(1)} all-gather(bf16[64,1536]{1,0:T(8,128)(2,1)S(1)} %get-tuple-element.52), channel_id=1, replica_groups=mesh['clips'=2,'row'=4,'col'=4] {'col'}, dimensions={0}, use_global_device_ids=true | all-gather | bytes 983040 | tf_op jit(solution)/shard_map/all_gather | solution.py:181
  405.6 2.6 convolution_convert_fusion.1
  408.4 18.2 %all_gather.29 = bf16[256,1536]{1,0:T(8,128)(2,1)S(1)} all-gather(bf16[64,1536]{1,0:T(8,128)(2,1)S(1)} %get-tuple-element.53), channel_id=1, replica_groups=mesh['clips'=2,'row'=4,'col'=4] {'col'}, dimensions={0}, use_global_device_ids=true | all-gather | bytes 983040 | tf_op jit(solution)/shard_map/all_gather | solution.py:181
  429.3 18.4 %all_gather.28 = bf16[256,1536]{1,0:T(8,128)(2,1)S(1)} all-gather(bf16[64,1536]{1,0:T(8,128)(2,1)S(1)} %get-tuple-element.51), channel_id=1, replica_groups=mesh['clips'=2,'row'=4,'col'=4] {'col'}, dimensions={0}, use_global_device_ids=true | all-gather | bytes 983040 | tf_op jit(solution)/shard_map/all_gather | solution.py:181
  447.7 2.6 convolution_convert_fusion.3
  455.2 7.4 %collective-permute-done.45 = bf16[64,3072]{1,0:T(8,128)(2,1)S(1)} collective-permute-done((bf16[64,3072]{1,0:T(8,128)(2,1)S(1)}, bf16[64,3072]{1,0:T(8,128)(2,1)S(1)}, u32[]{:S(2)}, u32[]{:S(2)}) %collective-permute-start.45) | collective-permute-done | bytes 393248 | tf_op jit(solution)/shard_map/ppermute | solution.py:101
  462.6 8.4 %collective-permute-done.39 = bf16[64,3072]{1,0:T(8,128)(2,1)S(1)} collective-permute-done((bf16[64,3072]{1,0:T(8,128)(2,1)S(1)}, bf16[64,3072]{1,0:T(8,128)(2,1)S(1)}, u32[]{:S(2)}, u32[]{:S(2)}) %collective-permute-start.39) | collective-permute-done | bytes 393248 | tf_op jit(solution)/shard_map/ppermute | solution.py:101
  471.0 8.4 %collective-permute-done.33 = bf16[64,3072]{1,0:T(8,128)(2,1)S(1)} collective-permute-done((bf16[64,3072]{1,0:T(8,128)(2,1)S(1)}, bf16[64,3072]{1,0:T(8,128)(2,1)S(1)}, u32[]{:S(2)}, u32[]{:S(2)}) %collective-permute-start.33) | collective-permute-done | bytes 393248 | tf_op jit(solution)/shard_map/ppermute | solution.py:101
  479.4 8.0 %collective-permute-done.27 = bf16[64,3072]{1,0:T(8,128)(2,1)S(1)} collective-permute-done((bf16[64,3072]{1,0:T(8,128)(2,1)S(1)}, bf16[64,3072]{1,0:T(8,128)(2,1)S(1)}, u32[]{:S(2)}, u32[]{:S(2)}) %collective-permute-start.27) | collective-permute-done | bytes 393248 | tf_op jit(solution)/shard_map/ppermute | solution.py:101
  493.2 8.0 %collective-permute-done.28 = bf16[64,3072]{1,0:T(8,128)(2,1)S(1)} collective-permute-done((bf16[64,3072]{1,0:T(8,128)(2,1)S(1)}, bf16[64,3072]{1,0:T(8,128)(2,1)S(1)}, u32[]{:S(2)}, u32[]{:S(2)}) %collective-permute-start.28) | collective-permute-done | bytes 393248 | tf_op jit(solution)/shard_map/ppermute | solution.py:101
  501.3 8.2 %collective-permute-done.34 = bf16[64,3072]{1,0:T(8,128)(2,1)S(1)} collective-permute-done((bf16[64,3072]{1,0:T(8,128)(2,1)S(1)}, bf16[64,3072]{1,0:T(8,128)(2,1)S(1)}, u32[]{:S(2)}, u32[]{:S(2)}) %collective-permute-start.34) | collective-permute-done | bytes 393248 | tf_op jit(solution)/shard_map/ppermute | solution.py:101
  509.8 8.2 %collective-permute-done.40 = bf16[64,3072]{1,0:T(8,128)(2,1)S(1)} collective-permute-done((bf16[64,3072]{1,0:T(8,128)(2,1)S(1)}, bf16[64,3072]{1,0:T(8,128)(2,1)S(1)}, u32[]{:S(2)}, u32[]{:S(2)}) %collective-permute-start.40) | collective-permute-done | bytes 393248 | tf_op jit(solution)/shard_map/ppermute | solution.py:101
  518.2 6.9 %collective-permute-done.46 = bf16[64,3072]{1,0:T(8,128)(2,1)S(1)} collective-permute-done((bf16[64,3072]{1,0:T(8,128)(2,1)S(1)}, bf16[64,3072]{1,0:T(8,128)(2,1)S(1)}, u32[]{:S(2)}, u32[]{:S(2)}) %collective-permute-start.46) | collective-permute-done | bytes 393248 | tf_op jit(solution)/shard_map/ppermute | solution.py:101
  529.8 2.6 convolution_multiply_fusion.2
  532.4 2.6 convolution_multiply_fusion.1
  535.1 2.9 convolution_multiply_fusion
  538.0 3.5 fusion.3
  541.6 22.3 %reduce-scatter.14.cloned.1.call-done = bf16[64,1536]{1,0:T(8,128)(2,1)} async-done(((bf16[256,1536]{1,0:T(8,128)(2,1)}), bf16[64,1536]{1,0:T(8,128)(2,1)}) %reduce-scatter.14.cloned.1.call-update) | async-done | bytes 196624 | tf_op jit(solution)/shard_map/reduce_scatter | solution.py:191
  563.9 4.9 add_convert_fusion
  (362 shorter events, 141.8 us)
Async XLA Ops:
  6.5 310.7 %reduce-scatter.12.cloned.1.call-start = ((), (), s32[]{:S(2)}) async-start(), calls=%async_computation.8 | async-start | bytes 983040 | tf_op jit(solution)/shard_map/reduce_scatter | solution.py:178
  32.1 75.4 %collective-permute-start.18 = (f32[2,256]{1,0:T(2,128)S(1)}, f32[2,256]{1,0:T(2,128)S(1)}, u32[]{:S(2)}, u32[]{:S(2)}) collective-permute-start(f32[2,256]{1,0:T(2,128)S(1)} %pad_maximum_fusion.3), channel_id=1, source_target_pairs={{0,4},{4,0},{8,12},{12,8},{1,5},{5,1},{9,13},{13,9},{2,6},{6,2},{1... | collective-permute-start | bytes 6152 | tf_op jit(solution)/shard_map/ppermute | solution.py:101
  50.6 58.5 %collective-permute-start.12 = (f32[2,256]{1,0:T(2,128)S(1)}, f32[2,256]{1,0:T(2,128)S(1)}, u32[]{:S(2)}, u32[]{:S(2)}) collective-permute-start(f32[2,256]{1,0:T(2,128)S(1)} %pad_maximum_fusion.2), channel_id=1, source_target_pairs={{0,4},{4,0},{8,12},{12,8},{1,5},{5,1},{9,13},{13,9},{2,6},{6,2},{1... | collective-permute-start | bytes 6152 | tf_op jit(solution)/shard_map/ppermute | solution.py:101
  69.7 40.0 %collective-permute-start.6 = (f32[2,256]{1,0:T(2,128)S(1)}, f32[2,256]{1,0:T(2,128)S(1)}, u32[]{:S(2)}, u32[]{:S(2)}) collective-permute-start(f32[2,256]{1,0:T(2,128)S(1)} %pad_maximum_fusion.1), channel_id=1, source_target_pairs={{0,4},{4,0},{8,12},{12,8},{1,5},{5,1},{9,13},{13,9},{2,6},{6,2},{1... | collective-permute-start | bytes 6152 | tf_op jit(solution)/shard_map/ppermute | solution.py:101
  90.1 21.3 %collective-permute-start = (f32[2,256]{1,0:T(2,128)S(1)}, f32[2,256]{1,0:T(2,128)S(1)}, u32[]{:S(2)}, u32[]{:S(2)}) collective-permute-start(f32[2,256]{1,0:T(2,128)S(1)} %pad_maximum_fusion), channel_id=1, source_target_pairs={{0,4},{4,0},{8,12},{12,8},{1,5},{5,1},{9,13},{13,9},{2,6},{6,2},{1... | collective-permute-start | bytes 6152 | tf_op jit(solution)/shard_map/ppermute | solution.py:101
  107.6 4.4 collective-permute-start.19
  109.2 19.7 %collective-permute-start.13 = (f32[2,256]{1,0:T(2,128)S(1)}, f32[2,256]{1,0:T(2,128)S(1)}, u32[]{:S(2)}, u32[]{:S(2)}) collective-permute-start(f32[2,256]{1,0:T(2,128)S(1)} %fusion.152), channel_id=1, source_target_pairs={{0,8},{4,12},{8,0},{12,4},{1,9},{5,13},{9,1},{13,5},{2,10},{6,14},... | collective-permute-start | bytes 6152 | tf_op jit(solution)/shard_map/ppermute | solution.py:101
  109.8 40.0 %collective-permute-start.7 = (f32[2,256]{1,0:T(2,128)S(1)}, f32[2,256]{1,0:T(2,128)S(1)}, u32[]{:S(2)}, u32[]{:S(2)}) collective-permute-start(f32[2,256]{1,0:T(2,128)S(1)} %fusion.153), channel_id=1, source_target_pairs={{0,8},{4,12},{8,0},{12,4},{1,9},{5,13},{9,1},{13,5},{2,10},{6,14},... | collective-permute-start | bytes 6152 | tf_op jit(solution)/shard_map/ppermute | solution.py:101
  111.4 58.8 %collective-permute-start.1 = (f32[2,256]{1,0:T(2,128)S(1)}, f32[2,256]{1,0:T(2,128)S(1)}, u32[]{:S(2)}, u32[]{:S(2)}) collective-permute-start(f32[2,256]{1,0:T(2,128)S(1)} %fusion.154), channel_id=1, source_target_pairs={{0,8},{4,12},{8,0},{12,4},{1,9},{5,13},{9,1},{13,5},{2,10},{6,14},... | collective-permute-start | bytes 6152 | tf_op jit(solution)/shard_map/ppermute | solution.py:101
  128.9 71.4 %collective-permute-start.20 = (bf16[2,3,256,256]{3,2,1,0:T(8,128)(2,1)}, bf16[2,3,256,256]{3,2,1,0:T(8,128)(2,1)}, u32[]{:S(2)}, u32[]{:S(2)}) collective-permute-start(bf16[2,3,256,256]{3,2,1,0:T(8,128)(2,1)} %bitcast.467), channel_id=1, source_target_pairs={{0,4},{4,0},{8,12},{12,8},{1,5},{5,1},{9,13},{13,9},{2,6},{6,2},{1... | collective-permute-start | bytes 2359304 | tf_op jit(solution)/shard_map/ppermute | solution.py:101
  149.4 53.5 %collective-permute-start.14 = (bf16[2,3,256,256]{3,2,1,0:T(8,128)(2,1)}, bf16[2,3,256,256]{3,2,1,0:T(8,128)(2,1)}, u32[]{:S(2)}, u32[]{:S(2)}) collective-permute-start(bf16[2,3,256,256]{3,2,1,0:T(8,128)(2,1)} %bitcast.468), channel_id=1, source_target_pairs={{0,4},{4,0},{8,12},{12,8},{1,5},{5,1},{9,13},{13,9},{2,6},{6,2},{1... | collective-permute-start | bytes 2359304 | tf_op jit(solution)/shard_map/ppermute | solution.py:101
  169.9 35.4 %collective-permute-start.8 = (bf16[2,3,256,256]{3,2,1,0:T(8,128)(2,1)}, bf16[2,3,256,256]{3,2,1,0:T(8,128)(2,1)}, u32[]{:S(2)}, u32[]{:S(2)}) collective-permute-start(bf16[2,3,256,256]{3,2,1,0:T(8,128)(2,1)} %bitcast.469), channel_id=1, source_target_pairs={{0,4},{4,0},{8,12},{12,8},{1,5},{5,1},{9,13},{13,9},{2,6},{6,2},{1... | collective-permute-start | bytes 2359304 | tf_op jit(solution)/shard_map/ppermute | solution.py:101
  189.8 18.8 %collective-permute-start.2 = (bf16[2,3,256,256]{3,2,1,0:T(8,128)(2,1)S(1)}, bf16[2,3,256,256]{3,2,1,0:T(8,128)(2,1)S(1)}, u32[]{:S(2)}, u32[]{:S(2)}) collective-permute-start(bf16[2,3,256,256]{3,2,1,0:T(8,128)(2,1)S(1)} %bitcast.529), channel_id=1, source_target_pairs={{0,4},{4,0},{8,12},{12,8},{1,5},{5,1},{9,13},{13,9},{2,6},{6,2},{1... | collective-permute-start | bytes 2359304 | tf_op jit(solution)/shard_map/ppermute | solution.py:101
  201.4 12.0 %collective-permute-start.21 = (bf16[3,256,256]{2,1,0:T(8,128)(2,1)S(1)}, bf16[3,256,256]{2,1,0:T(8,128)(2,1)S(1)}, u32[]{:S(2)}, u32[]{:S(2)}) collective-permute-start(bf16[3,256,256]{2,1,0:T(8,128)(2,1)S(1)} %fusion.89), channel_id=1, source_target_pairs={{0,8},{4,12},{8,0},{12,4},{1,9},{5,13},{9,1},{13,5},{2,10},{6,14},... | collective-permute-start | bytes 1179656 | tf_op jit(solution)/shard_map/ppermute | solution.py:101
  204.8 20.4 %collective-permute-start.15 = (bf16[3,256,256]{2,1,0:T(8,128)(2,1)}, bf16[3,256,256]{2,1,0:T(8,128)(2,1)}, u32[]{:S(2)}, u32[]{:S(2)}) collective-permute-start(bf16[3,256,256]{2,1,0:T(8,128)(2,1)} %fusion.92), channel_id=1, source_target_pairs={{0,8},{4,12},{8,0},{12,4},{1,9},{5,13},{9,1},{13,5},{2,10},{6,14},... | collective-permute-start | bytes 1179656 | tf_op jit(solution)/shard_map/ppermute | solution.py:101
  207.2 53.0 %collective-permute-start.9 = (bf16[3,256,256]{2,1,0:T(8,128)(2,1)}, bf16[3,256,256]{2,1,0:T(8,128)(2,1)}, u32[]{:S(2)}, u32[]{:S(2)}) collective-permute-start(bf16[3,256,256]{2,1,0:T(8,128)(2,1)} %fusion.95), channel_id=1, source_target_pairs={{0,8},{4,12},{8,0},{12,4},{1,9},{5,13},{9,1},{13,5},{2,10},{6,14},... | collective-permute-start | bytes 1179656 | tf_op jit(solution)/shard_map/ppermute | solution.py:101
  209.6 73.4 %collective-permute-start.3 = (bf16[3,256,256]{2,1,0:T(8,128)(2,1)}, bf16[3,256,256]{2,1,0:T(8,128)(2,1)}, u32[]{:S(2)}, u32[]{:S(2)}) collective-permute-start(bf16[3,256,256]{2,1,0:T(8,128)(2,1)} %fusion.98), channel_id=1, source_target_pairs={{0,8},{4,12},{8,0},{12,4},{1,9},{5,13},{9,1},{13,5},{2,10},{6,14},... | collective-permute-start | bytes 1179656 | tf_op jit(solution)/shard_map/ppermute | solution.py:101
  222.8 18.0 %collective-permute-start.22 = (bf16[256,256]{1,0:T(8,128)(2,1)}, bf16[256,256]{1,0:T(8,128)(2,1)S(1)}, u32[]{:S(2)}, u32[]{:S(2)}) collective-permute-start(bf16[256,256]{1,0:T(8,128)(2,1)} %copy.101), channel_id=1, source_target_pairs={{0,8},{4,12},{8,0},{12,4},{1,9},{5,13},{9,1},{13,5},{2,10},{6,14},... | collective-permute-start | bytes 393224 | tf_op jit(solution)/shard_map/ppermute | solution.py:101
  241.6 4.1 collective-permute-start.23
  252.8 64.5 %reduce-scatter.10.cloned.1.call-start = ((), (), s32[]{:S(2)}) async-start(), calls=%async_computation.7 | async-start | bytes 983040 | tf_op jit(solution)/shard_map/reduce_scatter | solution.py:178
  257.8 6.1 %collective-permute-start.16 = (bf16[256,256]{1,0:T(8,128)(2,1)}, bf16[256,256]{1,0:T(8,128)(2,1)S(1)}, u32[]{:S(2)}, u32[]{:S(2)}) collective-permute-start(bf16[256,256]{1,0:T(8,128)(2,1)} %copy.83), channel_id=1, source_target_pairs={{0,8},{4,12},{8,0},{12,4},{1,9},{5,13},{9,1},{13,5},{2,10},{6,14},... | collective-permute-start | bytes 393224 | tf_op jit(solution)/shard_map/ppermute | solution.py:101
  264.6 4.1 collective-permute-start.17
  275.7 50.2 %reduce-scatter.8.cloned.1.call-start = ((), (), s32[]{:S(2)}) async-start(), calls=%async_computation.6 | async-start | bytes 983040 | tf_op jit(solution)/shard_map/reduce_scatter | solution.py:178
  280.7 6.1 %collective-permute-start.10 = (bf16[256,256]{1,0:T(8,128)(2,1)}, bf16[256,256]{1,0:T(8,128)(2,1)S(1)}, u32[]{:S(2)}, u32[]{:S(2)}) collective-permute-start(bf16[256,256]{1,0:T(8,128)(2,1)} %copy.65), channel_id=1, source_target_pairs={{0,8},{4,12},{8,0},{12,4},{1,9},{5,13},{9,1},{13,5},{2,10},{6,14},... | collective-permute-start | bytes 393224 | tf_op jit(solution)/shard_map/ppermute | solution.py:101
  287.5 5.1 collective-permute-start.11
  299.7 51.0 %reduce-scatter.6.cloned.1.call-start = ((), (), s32[]{:S(2)}) async-start(), calls=%async_computation.5 | async-start | bytes 983040 | tf_op jit(solution)/shard_map/reduce_scatter | solution.py:178
  301.5 6.1 %collective-permute-start.4 = (bf16[256,256]{1,0:T(8,128)(2,1)}, bf16[256,256]{1,0:T(8,128)(2,1)S(1)}, u32[]{:S(2)}, u32[]{:S(2)}) collective-permute-start(bf16[256,256]{1,0:T(8,128)(2,1)} %copy.48), channel_id=1, source_target_pairs={{0,8},{4,12},{8,0},{12,4},{1,9},{5,13},{9,1},{13,5},{2,10},{6,14},... | collective-permute-start | bytes 393224 | tf_op jit(solution)/shard_map/ppermute | solution.py:101
  317.2 246.7 %reduce-scatter.14.cloned.1.call-start = ((), (), s32[]{:S(2)}) async-start(), calls=%async_computation.9 | async-start | bytes 983040 | tf_op jit(solution)/shard_map/reduce_scatter | solution.py:191
  353.4 4.2 collective-permute-start.24
  353.9 4.4 collective-permute-start.43
  355.4 3.6 collective-permute-start.31
  356.1 3.6 collective-permute-start.37
  357.6 3.6 collective-permute-start.25
  386.4 64.1 %collective-permute-start.44 = (bf16[2,64,3072]{2,1,0:T(8,128)(2,1)S(1)}, bf16[2,64,3072]{2,1,0:T(8,128)(2,1)S(1)}, u32[]{:S(2)}, u32[]{:S(2)}) collective-permute-start(bf16[2,64,3072]{2,1,0:T(8,128)(2,1)S(1)} %dynamic-slice_bitcast_fusion), channel_id=1, source_target_pairs={{0,4},{4,0},{8,12},{12,8},{1,5},{5,1},{9,13},{13,9},{2,6},{6,2},{1... | collective-permute-start | bytes 2359304 | tf_op jit(solution)/shard_map/ppermute | solution.py:101
  408.3 42.8 %collective-permute-start.38 = (bf16[2,64,3072]{2,1,0:T(8,128)(2,1)S(1)}, bf16[2,64,3072]{2,1,0:T(8,128)(2,1)S(1)}, u32[]{:S(2)}, u32[]{:S(2)}) collective-permute-start(bf16[2,64,3072]{2,1,0:T(8,128)(2,1)S(1)} %dynamic-slice_bitcast_fusion.1), channel_id=1, source_target_pairs={{0,4},{4,0},{8,12},{12,8},{1,5},{5,1},{9,13},{13,9},{2,6},{6,2},{1... | collective-permute-start | bytes 2359304 | tf_op jit(solution)/shard_map/ppermute | solution.py:101
  429.2 23.6 %collective-permute-start.32 = (bf16[2,64,3072]{2,1,0:T(8,128)(2,1)S(1)}, bf16[2,64,3072]{2,1,0:T(8,128)(2,1)S(1)}, u32[]{:S(2)}, u32[]{:S(2)}) collective-permute-start(bf16[2,64,3072]{2,1,0:T(8,128)(2,1)S(1)} %dynamic-slice_bitcast_fusion.2), channel_id=1, source_target_pairs={{0,4},{4,0},{8,12},{12,8},{1,5},{5,1},{9,13},{13,9},{2,6},{6,2},{1... | collective-permute-start | bytes 2359304 | tf_op jit(solution)/shard_map/ppermute | solution.py:101
  450.4 3.1 collective-permute-start.26
  450.6 12.0 %collective-permute-start.45 = (bf16[64,3072]{1,0:T(8,128)(2,1)S(1)}, bf16[64,3072]{1,0:T(8,128)(2,1)S(1)}, u32[]{:S(2)}, u32[]{:S(2)}) collective-permute-start(bf16[64,3072]{1,0:T(8,128)(2,1)S(1)} %fusion.77), channel_id=1, source_target_pairs={{0,8},{4,12},{8,0},{12,4},{1,9},{5,13},{9,1},{13,5},{2,10},{6,14},... | collective-permute-start | bytes 1179656 | tf_op jit(solution)/shard_map/ppermute | solution.py:101
  451.2 19.8 %collective-permute-start.39 = (bf16[64,3072]{1,0:T(8,128)(2,1)S(1)}, bf16[64,3072]{1,0:T(8,128)(2,1)S(1)}, u32[]{:S(2)}, u32[]{:S(2)}) collective-permute-start(bf16[64,3072]{1,0:T(8,128)(2,1)S(1)} %fusion.80), channel_id=1, source_target_pairs={{0,8},{4,12},{8,0},{12,4},{1,9},{5,13},{9,1},{13,5},{2,10},{6,14},... | collective-permute-start | bytes 1179656 | tf_op jit(solution)/shard_map/ppermute | solution.py:101
  452.9 26.5 %collective-permute-start.33 = (bf16[64,3072]{1,0:T(8,128)(2,1)S(1)}, bf16[64,3072]{1,0:T(8,128)(2,1)S(1)}, u32[]{:S(2)}, u32[]{:S(2)}) collective-permute-start(bf16[64,3072]{1,0:T(8,128)(2,1)S(1)} %fusion.83), channel_id=1, source_target_pairs={{0,8},{4,12},{8,0},{12,4},{1,9},{5,13},{9,1},{13,5},{2,10},{6,14},... | collective-permute-start | bytes 1179656 | tf_op jit(solution)/shard_map/ppermute | solution.py:101
  453.6 33.8 %collective-permute-start.27 = (bf16[64,3072]{1,0:T(8,128)(2,1)S(1)}, bf16[64,3072]{1,0:T(8,128)(2,1)S(1)}, u32[]{:S(2)}, u32[]{:S(2)}) collective-permute-start(bf16[64,3072]{1,0:T(8,128)(2,1)S(1)} %fusion.86), channel_id=1, source_target_pairs={{0,8},{4,12},{8,0},{12,4},{1,9},{5,13},{9,1},{13,5},{2,10},{6,14},... | collective-permute-start | bytes 1179656 | tf_op jit(solution)/shard_map/ppermute | solution.py:101
  489.0 12.1 %collective-permute-start.28 = (bf16[64,3072]{1,0:T(8,128)(2,1)S(1)}, bf16[64,3072]{1,0:T(8,128)(2,1)S(1)}, u32[]{:S(2)}, u32[]{:S(2)}) collective-permute-start(bf16[64,3072]{1,0:T(8,128)(2,1)S(1)} %get-tuple-element.71), channel_id=1, source_target_pairs={{0,8},{4,12},{8,0},{12,4},{1,9},{5,13},{9,1},{13,5},{2,10},{6,14},... | collective-permute-start | bytes 1179656 | tf_op jit(solution)/shard_map/ppermute | solution.py:101
  489.6 20.0 %collective-permute-start.34 = (bf16[64,3072]{1,0:T(8,128)(2,1)S(1)}, bf16[64,3072]{1,0:T(8,128)(2,1)S(1)}, u32[]{:S(2)}, u32[]{:S(2)}) collective-permute-start(bf16[64,3072]{1,0:T(8,128)(2,1)S(1)} %get-tuple-element.72), channel_id=1, source_target_pairs={{0,8},{4,12},{8,0},{12,4},{1,9},{5,13},{9,1},{13,5},{2,10},{6,14},... | collective-permute-start | bytes 1179656 | tf_op jit(solution)/shard_map/ppermute | solution.py:101
  491.1 26.9 %collective-permute-start.40 = (bf16[64,3072]{1,0:T(8,128)(2,1)S(1)}, bf16[64,3072]{1,0:T(8,128)(2,1)S(1)}, u32[]{:S(2)}, u32[]{:S(2)}) collective-permute-start(bf16[64,3072]{1,0:T(8,128)(2,1)S(1)} %get-tuple-element.73), channel_id=1, source_target_pairs={{0,8},{4,12},{8,0},{12,4},{1,9},{5,13},{9,1},{13,5},{2,10},{6,14},... | collective-permute-start | bytes 1179656 | tf_op jit(solution)/shard_map/ppermute | solution.py:101
  491.6 33.5 %collective-permute-start.46 = (bf16[64,3072]{1,0:T(8,128)(2,1)S(1)}, bf16[64,3072]{1,0:T(8,128)(2,1)S(1)}, u32[]{:S(2)}, u32[]{:S(2)}) collective-permute-start(bf16[64,3072]{1,0:T(8,128)(2,1)S(1)} %get-tuple-element.74), channel_id=1, source_target_pairs={{0,8},{4,12},{8,0},{12,4},{1,9},{5,13},{9,1},{13,5},{2,10},{6,14},... | collective-permute-start | bytes 1179656 | tf_op jit(solution)/shard_map/ppermute | solution.py:101
  501.3 26.7 %collective-permute-start.29 = (bf16[2,64,3072]{2,1,0:T(8,128)(2,1)S(1)}, bf16[2,64,3072]{2,1,0:T(8,128)(2,1)S(1)}, u32[]{:S(2)}, u32[]{:S(2)}) collective-permute-start(bf16[2,64,3072]{2,1,0:T(8,128)(2,1)S(1)} %maximum_select_fusion.4), channel_id=1, source_target_pairs={{0,4},{4,0},{8,12},{12,8},{1,5},{5,1},{9,13},{13,9},{2,6},{6,2},{1... | collective-permute-start | bytes 2359304 | tf_op jit(solution)/shard_map/ppermute | solution.py:101
  509.7 16.2 %collective-permute-start.35 = (bf16[2,64,3072]{2,1,0:T(8,128)(2,1)S(1)}, bf16[2,64,3072]{2,1,0:T(8,128)(2,1)S(1)}, u32[]{:S(2)}, u32[]{:S(2)}) collective-permute-start(bf16[2,64,3072]{2,1,0:T(8,128)(2,1)S(1)} %maximum_select_fusion.6), channel_id=1, source_target_pairs={{0,4},{4,0},{8,12},{12,8},{1,5},{5,1},{9,13},{13,9},{2,6},{6,2},{1... | collective-permute-start | bytes 2359304 | tf_op jit(solution)/shard_map/ppermute | solution.py:101
  518.1 8.2 %collective-permute-start.41 = (bf16[2,64,3072]{2,1,0:T(8,128)(2,1)S(1)}, bf16[2,64,3072]{2,1,0:T(8,128)(2,1)S(1)}, u32[]{:S(2)}, u32[]{:S(2)}) collective-permute-start(bf16[2,64,3072]{2,1,0:T(8,128)(2,1)S(1)} %maximum_select_fusion.7), channel_id=1, source_target_pairs={{0,4},{4,0},{8,12},{12,8},{1,5},{5,1},{9,13},{13,9},{2,6},{6,2},{1... | collective-permute-start | bytes 2359304 | tf_op jit(solution)/shard_map/ppermute | solution.py:101
  (58 other events, 958.7 us)
Sparse Core Ops, SparseCore 0:
  252.9 23.0 reduce-scatter.11
  278.3 22.5 reduce-scatter.9
  303.3 22.5 reduce-scatter.7
  328.0 22.5 reduce-scatter.5
  541.7 22.1 reduce-scatter.13
where the time goes:
time: 580 us; the launch traced here: 576 us
  waiting for transfers between devices  151 us (26%)
  blocking collectives  149 us (26%)
  local copies, waits for them, and re-layouts  101 us (17%)
  matrix products  89.1 us (15%)
  other arithmetic  40.9 us (7%)
  starting transfers between devices  30 us (5%)
  between operations  14.7 us (3%)
    ppermute x48, waiting for transfers between devices, swap_row(): return lax.ppermute(value, 'row', [(r, r ^ distance) for r in range(size)])  95.6 us
    all_gather x4, blocking collectives, branch_layer(): x_all = lax.all_gather(x, 'col', axis=0, tiled=True).astype(jnp.float32)  76.1 us
    all_gather x4, blocking collectives, branch_layer(): second_all = lax.all_gather(second, 'col', axis=0, tiled=True)  72.7 us
    dot_general x4, matrix products, branch_layer(): jnp.dot(first, w_flat, preferred_element_type=jnp.float32).astype(BF)  40.9 us
    reduce_scatter x4, waiting for transfers between devices, branch_layer(): out = lax.psum_scatter(partial, 'col', scatter_dimension=0, tiled=True)  33.3 us
    ppermute x48, starting transfers between devices, swap_row(): return lax.ppermute(value, 'row', [(r, r ^ distance) for r in range(size)])  29.9 us
    reduce_scatter x1, waiting for transfers between devices, branch_layer(): lax.psum_scatter(total.astype(BF), 'col', scatter_dimension=0, tiled=True)  22.3 us
    unnamed x111, local copies, waits for them, and re-layouts  21.5 us
  transfers between devices with their start and end apart: 53, of which 22 were waited for; matrix products, arithmetic and copies ran while one was open for 34% of the time, Pallas kernels for 0%

commit v1 on v0

--- a/solution.py
+++ b/solution.py
@@ -178,7 +178,14 @@
         out = lax.psum_scatter(partial, "col", scatter_dimension=0, tiled=True)
         resid = x.astype(jnp.float32) + modulation[b, 2][None] * out.astype(jnp.float32)
         second = apply_norm(resid, sum_over_row(moments(resid)), modulation[b, 3], modulation[b, 4])
-        second_all = lax.all_gather(second, "col", axis=0, tiled=True)
+        ring = [second]
+        for hop in range(3):
+            ring.append(lax.ppermute(ring[-1], "col", [(dev, (dev + 1) % 4) for dev in range(4)]))
+        second_all = jnp.roll(
+            jnp.concatenate(ring[::-1], axis=0),
+            (lax.axis_index("col") + 1) * ring[0].shape[0],
+            axis=0,
+        )
         partial = jnp.dot(second_all, w_up, preferred_element_type=jnp.float32).astype(BF)
         up = scatter_row(partial.reshape(2, 2, tokens // 4, -1))
         act = jax.nn.gelu(up + up_bias[None], approximate=True).astype(BF)

time: 580 us -> 563 us (0.971)
  blocking collectives: 149 us -> 76.1 us
  waiting for transfers between devices: 151 us -> 187 us
  matrix products: 89.1 us -> 101 us
    all_gather x4 -> x0, blocking collectives: 72.7 us -> none  [branch_layer(): second_all = lax.all_gather(second, 'col', axis=0, tiled=True)]
    ppermute x0 -> x12, waiting for transfers between devices: none -> 37.8 us  [branch_layer(): lax.ppermute(ring[-1], 'col', [(dev, (dev + 1) % 4) for dev in range(4)])]
    dot_general x4, matrix products: 14.2 us -> 25.6 us  [branch_layer(): jnp.dot(second_all, w_up, preferred_element_type=jnp.float32).astype(BF)]
    unnamed x111 -> x135, local copies, waits for them, and re-layouts: 21.5 us -> 23.2 us
  transfers between devices with their start and end apart: 53 -> 65, of which waited for: 22 -> 31; matrix products, arithmetic and copies ran while one was open for 34% -> 38% of each run, Pallas kernels for 0% -> 0%
where the time goes in v1:
time: 563 us; the launch traced here: 558 us
  waiting for transfers between devices  187 us (33%)
  local copies, waits for them, and re-layouts  102 us (18%)
  matrix products  101 us (18%)
  blocking collectives  76.1 us (14%)
  other arithmetic  41 us (7%)
  starting transfers between devices  35.3 us (6%)
  between operations  14.9 us (3%)
    ppermute x48, waiting for transfers between devices, swap_row(): return lax.ppermute(value, 'row', [(r, r ^ distance) for r in range(size)])  95.6 us
    all_gather x4, blocking collectives, branch_layer(): x_all = lax.all_gather(x, 'col', axis=0, tiled=True).astype(jnp.float32)  76.1 us
    dot_general x4, matrix products, branch_layer(): jnp.dot(first, w_flat, preferred_element_type=jnp.float32).astype(BF)  40.9 us
    ppermute x12, waiting for transfers between devices, branch_layer(): lax.ppermute(ring[-1], 'col', [(dev, (dev + 1) % 4) for dev in range(4)])  37.8 us
    reduce_scatter x4, waiting for transfers between devices, branch_layer(): out = lax.psum_scatter(partial, 'col', scatter_dimension=0, tiled=True)  33.2 us
    ppermute x48, starting transfers between devices, swap_row(): return lax.ppermute(value, 'row', [(r, r ^ distance) for r in range(size)])  30 us
    dot_general x4, matrix products, branch_layer(): jnp.dot(second_all, w_up, preferred_element_type=jnp.float32).astype(BF)  25.6 us
    unnamed x135, local copies, waits for them, and re-layouts  23.2 us
  transfers between devices with their start and end apart: 65, of which 31 were waited for; matrix products, arithmetic and copies ran while one was open for 38% of the time, Pallas kernels for 0%

profile of v1, /device:TPU:0, one launch (start us, length us, event | category | flops | bytes accessed | tf_op | source)
XLA Modules:
  0.0 557.9 jit_solution(15167379390504259466)
XLA Ops:
  10.4 21.3 %all-gather.3 = bf16[1,256,1536]{2,1,0:T(8,128)(2,1)S(1)} all-gather(bf16[1,64,1536]{2,1,0:T(8,128)(2,1)S(1)} %get-tuple-element.57), channel_id=5, replica_groups=mesh['clips'=2,'row'=4,'col'=4] {'col'}, dimensions={1}, use_global_device_ids=true | all-gather | bytes 983040 | tf_op jit(solution)/shard_map/all_gather | solution.py:169
  32.2 18.0 %all-gather.2 = bf16[1,256,1536]{2,1,0:T(8,128)(2,1)S(1)} all-gather(bf16[1,64,1536]{2,1,0:T(8,128)(2,1)S(1)} %get-tuple-element.56), channel_id=4, replica_groups=mesh['clips'=2,'row'=4,'col'=4] {'col'}, dimensions={1}, use_global_device_ids=true | all-gather | bytes 983040 | tf_op jit(solution)/shard_map/all_gather | solution.py:169
  51.1 18.1 %all-gather.1 = bf16[1,256,1536]{2,1,0:T(8,128)(2,1)S(1)} all-gather(bf16[1,64,1536]{2,1,0:T(8,128)(2,1)S(1)} %get-tuple-element.58), channel_id=3, replica_groups=mesh['clips'=2,'row'=4,'col'=4] {'col'}, dimensions={1}, use_global_device_ids=true | all-gather | bytes 983040 | tf_op jit(solution)/shard_map/all_gather | solution.py:169
  70.1 18.7 %all-gather = bf16[1,256,1536]{2,1,0:T(8,128)(2,1)S(1)} all-gather(bf16[1,64,1536]{2,1,0:T(8,128)(2,1)S(1)} %get-tuple-element.59), channel_id=2, replica_groups=mesh['clips'=2,'row'=4,'col'=4] {'col'}, dimensions={1}, use_global_device_ids=true | all-gather | bytes 983040 | tf_op jit(solution)/shard_map/all_gather | solution.py:169
  94.8 12.7 %copy.38 = bf16[1536,3,1024]{0,2,1:T(8,128)(2,1)} copy(bf16[1536,3,1024]{2,0,1:T(8,128)(2,1)} %param.12) | data formatting | bytes 18874368 | tf_op args[2]
  111.9 7.8 %convolution_convert_fusion.4 = bf16[256,3072]{1,0:T(8,128)(2,1)} fusion(bf16[1536,3072]{0,1:T(8,128)(2,1)} %bitcast.473, bf16[1,256,1536]{2,1,0:T(8,128)(2,1)} %copy-done.14, f32[1536]{0:T(1024)S(1)} %get-tuple-element.30, f32[1536]{0:T(1024)S(1)} %get-tuple-element.31, f32[256]{0:T(256)S(1)} %add_rsqrt_fusion, f32[256]{0:T(256)S(1)} %bitcast.605), kind=kOutput, calls=%fused_computation.4 | convolution fusion | flops 2419064832 | bytes 11810816 | tf_op jit(solution)/shard_map/dot_general | solution.py:172
  119.8 5.0 reshape.1011
  124.8 3.0 constant_dynamic-slice_fusion.1
  129.2 11.0 %convolution_convert_fusion.5 = bf16[256,3072]{1,0:T(8,128)(2,1)} fusion(bf16[1536,3072]{0,1:T(8,128)(2,1)} %bitcast.474, bf16[1,256,1536]{2,1,0:T(8,128)(2,1)S(1)} %copy-done.13, f32[1536]{0:T(1024)S(1)} %get-tuple-element.33, f32[1536]{0:T(1024)S(1)} %get-tuple-element.34, f32[256]{0:T(256)S(1)} %add_rsqrt_fusion.1, f32[256]{0:T(256)S(1)} %bitcast.607), kind=kOutput, calls=%fused_computation.5 | convolution fusion | flops 2419064832 | bytes 11810816 | tf_op jit(solution)/shard_map/dot_general | solution.py:172
  140.2 5.2 reshape.1009
  145.3 3.0 constant_dynamic-slice_fusion.4
  149.7 11.0 %convolution_convert_fusion.6 = bf16[256,3072]{1,0:T(8,128)(2,1)} fusion(bf16[1536,3072]{0,1:T(8,128)(2,1)} %bitcast.475, bf16[1,256,1536]{2,1,0:T(8,128)(2,1)S(1)} %copy-done.11, f32[1536]{0:T(1024)S(1)} %get-tuple-element.37, f32[1536]{0:T(1024)S(1)} %get-tuple-element.38, f32[256]{0:T(256)S(1)} %add_rsqrt_fusion.2, f32[256]{0:T(256)S(1)} %bitcast.609), kind=kOutput, calls=%fused_computation.6 | convolution fusion | flops 2419064832 | bytes 11810816 | tf_op jit(solution)/shard_map/dot_general | solution.py:172
  160.8 5.0 reshape.1007
  165.8 3.0 constant_dynamic-slice_fusion.7
  170.1 11.0 %convolution_convert_fusion.7 = bf16[256,3072]{1,0:T(8,128)(2,1)} fusion(bf16[1536,3072]{0,1:T(8,128)(2,1)} %bitcast.476, bf16[1,256,1536]{2,1,0:T(8,128)(2,1)S(1)} %copy-done.9, f32[1536]{0:T(1024)S(1)} %get-tuple-element.40, f32[1536]{0:T(1024)S(1)} %get-tuple-element.41, f32[256]{0:T(256)S(1)} %add_rsqrt_fusion.3, f32[256]{0:T(256)S(1)} %bitcast.603), kind=kOutput, calls=%fused_computation.7 | convolution fusion | flops 2419064832 | bytes 11810816 | tf_op jit(solution)/shard_map/dot_general | solution.py:172
  181.2 5.2 reshape.1005
  186.4 3.0 constant_dynamic-slice_fusion.10
  209.9 3.2 collective-permute-done.21
  226.5 14.1 %collective-permute-done.22 = bf16[256,256]{1,0:T(8,128)(2,1)S(1)} collective-permute-done((bf16[256,256]{1,0:T(8,128)(2,1)}, bf16[256,256]{1,0:T(8,128)(2,1)S(1)}, u32[]{:S(2)}, u32[]{:S(2)}) %collective-permute-start.22) | collective-permute-done | bytes 131104 | tf_op jit(solution)/shard_map/ppermute | solution.py:101
  249.5 3.4 convolution_convert_fusion.8
  272.8 3.0 convolution_convert_fusion.9
  303.3 4.5 collective-permute-done.4
  317.5 8.4 %reduce-scatter.8.cloned.1.call-done = bf16[64,1536]{1,0:T(8,128)(2,1)} async-done(((bf16[256,1536]{1,0:T(8,128)(2,1)}), bf16[64,1536]{1,0:T(8,128)(2,1)}) %reduce-scatter.8.cloned.1.call-update) | async-done | bytes 196624 | tf_op jit(solution)/shard_map/reduce_scatter | solution.py:178
  325.9 24.8 %reduce-scatter.6.cloned.1.call-done = bf16[64,1536]{1,0:T(8,128)(2,1)} async-done(((bf16[256,1536]{1,0:T(8,128)(2,1)}), bf16[64,1536]{1,0:T(8,128)(2,1)}) %reduce-scatter.6.cloned.1.call-update) | async-done | bytes 196624 | tf_op jit(solution)/shard_map/reduce_scatter | solution.py:178
  367.2 4.3 collective-permute-done.53
  371.5 4.2 collective-permute-done.44
  375.7 4.2 collective-permute-done.35
  379.9 4.2 collective-permute-done.26
  384.1 4.2 collective-permute-done.54
  388.3 4.3 collective-permute-done.45
  392.7 4.2 collective-permute-done.36
  396.9 4.2 collective-permute-done.27
  401.3 3.9 collective-permute-done.55
  405.2 7.8 %convolution_convert_fusion = bf16[256,3072]{1,0:T(8,128)(2,1)S(1)} fusion(bf16[1536,3072]{1,0:T(8,128)(2,1)} %param.14, s32[]{:T(128)S(6)} %select_n.373, bf16[64,1536]{1,0:T(8,128)(2,1)S(1)} %collective-permute-done.55, bf16[64,1536]{1,0:T(8,128)(2,1)S(1)} %collective-permute-done.54, bf16[64,1536]{1,0:T(8,128)(2,1)} %copy-done.55, ...), kind=kOutput, calls=%fused_computation | convolution fusion | flops 2422996992 | bytes 11796484 | tf_op jit(solution)/shard_map/dot_general | solution.py:189
  414.1 7.7 %convolution_convert_fusion.1 = bf16[256,3072]{1,0:T(8,128)(2,1)S(1)} fusion(bf16[1536,3072]{1,0:T(8,128)(2,1)} %param.14, s32[]{:T(128)S(6)} %select_n.373, bf16[64,1536]{1,0:T(8,128)(2,1)S(1)} %collective-permute-done.46, bf16[64,1536]{1,0:T(8,128)(2,1)} %collective-permute-done.45, bf16[64,1536]{1,0:T(8,128)(2,1)S(1)} %copy-done.57, ...), kind=kOutput, calls=%fused_computation.1 | convolution fusion | flops 2422996992 | bytes 11796484 | tf_op jit(solution)/shard_map/dot_general | solution.py:189
  422.8 5.0 convolution_convert_fusion.2
  428.8 5.2 convolution_convert_fusion.3
  438.9 7.3 %collective-permute-done.57 = bf16[64,3072]{1,0:T(8,128)(2,1)S(1)} collective-permute-done((bf16[64,3072]{1,0:T(8,128)(2,1)S(1)}, bf16[64,3072]{1,0:T(8,128)(2,1)S(1)}, u32[]{:S(2)}, u32[]{:S(2)}) %collective-permute-start.57) | collective-permute-done | bytes 393248 | tf_op jit(solution)/shard_map/ppermute | solution.py:101
  446.2 8.4 %collective-permute-done.48 = bf16[64,3072]{1,0:T(8,128)(2,1)S(1)} collective-permute-done((bf16[64,3072]{1,0:T(8,128)(2,1)S(1)}, bf16[64,3072]{1,0:T(8,128)(2,1)S(1)}, u32[]{:S(2)}, u32[]{:S(2)}) %collective-permute-start.48) | collective-permute-done | bytes 393248 | tf_op jit(solution)/shard_map/ppermute | solution.py:101
  454.6 8.4 %collective-permute-done.39 = bf16[64,3072]{1,0:T(8,128)(2,1)S(1)} collective-permute-done((bf16[64,3072]{1,0:T(8,128)(2,1)S(1)}, bf16[64,3072]{1,0:T(8,128)(2,1)S(1)}, u32[]{:S(2)}, u32[]{:S(2)}) %collective-permute-start.39) | collective-permute-done | bytes 393248 | tf_op jit(solution)/shard_map/ppermute | solution.py:101
  463.1 8.0 %collective-permute-done.30 = bf16[64,3072]{1,0:T(8,128)(2,1)S(1)} collective-permute-done((bf16[64,3072]{1,0:T(8,128)(2,1)S(1)}, bf16[64,3072]{1,0:T(8,128)(2,1)S(1)}, u32[]{:S(2)}, u32[]{:S(2)}) %collective-permute-start.30) | collective-permute-done | bytes 393248 | tf_op jit(solution)/shard_map/ppermute | solution.py:101
  476.8 8.0 %collective-permute-done.31 = bf16[64,3072]{1,0:T(8,128)(2,1)S(1)} collective-permute-done((bf16[64,3072]{1,0:T(8,128)(2,1)S(1)}, bf16[64,3072]{1,0:T(8,128)(2,1)S(1)}, u32[]{:S(2)}, u32[]{:S(2)}) %collective-permute-start.31) | collective-permute-done | bytes 393248 | tf_op jit(solution)/shard_map/ppermute | solution.py:101
  485.0 8.2 %collective-permute-done.40 = bf16[64,3072]{1,0:T(8,128)(2,1)S(1)} collective-permute-done((bf16[64,3072]{1,0:T(8,128)(2,1)S(1)}, bf16[64,3072]{1,0:T(8,128)(2,1)S(1)}, u32[]{:S(2)}, u32[]{:S(2)}) %collective-permute-start.40) | collective-permute-done | bytes 393248 | tf_op jit(solution)/shard_map/ppermute | solution.py:101
  493.4 8.2 %collective-permute-done.49 = bf16[64,3072]{1,0:T(8,128)(2,1)S(1)} collective-permute-done((bf16[64,3072]{1,0:T(8,128)(2,1)S(1)}, bf16[64,3072]{1,0:T(8,128)(2,1)S(1)}, u32[]{:S(2)}, u32[]{:S(2)}) %collective-permute-start.49) | collective-permute-done | bytes 393248 | tf_op jit(solution)/shard_map/ppermute | solution.py:101
  501.9 6.9 %collective-permute-done.58 = bf16[64,3072]{1,0:T(8,128)(2,1)S(1)} collective-permute-done((bf16[64,3072]{1,0:T(8,128)(2,1)S(1)}, bf16[64,3072]{1,0:T(8,128)(2,1)S(1)}, u32[]{:S(2)}, u32[]{:S(2)}) %collective-permute-start.58) | collective-permute-done | bytes 393248 | tf_op jit(solution)/shard_map/ppermute | solution.py:101
  521.7 3.6 fusion.3
  525.3 20.9 %reduce-scatter.14.cloned.1.call-done = bf16[64,1536]{1,0:T(8,128)(2,1)} async-done(((bf16[256,1536]{1,0:T(8,128)(2,1)}), bf16[64,1536]{1,0:T(8,128)(2,1)}) %reduce-scatter.14.cloned.1.call-update) | async-done | bytes 196624 | tf_op jit(solution)/shard_map/reduce_scatter | solution.py:198
  546.1 5.0 add_convert_fusion
  (406 shorter events, 163.1 us)
Async XLA Ops:
  6.5 310.9 %reduce-scatter.12.cloned.1.call-start = ((), (), s32[]{:S(2)}) async-start(), calls=%async_computation.8 | async-start | bytes 983040 | tf_op jit(solution)/shard_map/reduce_scatter | solution.py:178
  32.1 75.4 %collective-permute-start.18 = (f32[2,256]{1,0:T(2,128)S(1)}, f32[2,256]{1,0:T(2,128)S(1)}, u32[]{:S(2)}, u32[]{:S(2)}) collective-permute-start(f32[2,256]{1,0:T(2,128)S(1)} %pad_maximum_fusion.3), channel_id=1, source_target_pairs={{0,4},{4,0},{8,12},{12,8},{1,5},{5,1},{9,13},{13,9},{2,6},{6,2},{1... | collective-permute-start | bytes 6152 | tf_op jit(solution)/shard_map/ppermute | solution.py:101
  50.6 58.5 %collective-permute-start.12 = (f32[2,256]{1,0:T(2,128)S(1)}, f32[2,256]{1,0:T(2,128)S(1)}, u32[]{:S(2)}, u32[]{:S(2)}) collective-permute-start(f32[2,256]{1,0:T(2,128)S(1)} %pad_maximum_fusion.2), channel_id=1, source_target_pairs={{0,4},{4,0},{8,12},{12,8},{1,5},{5,1},{9,13},{13,9},{2,6},{6,2},{1... | collective-permute-start | bytes 6152 | tf_op jit(solution)/shard_map/ppermute | solution.py:101
  69.6 40.1 %collective-permute-start.6 = (f32[2,256]{1,0:T(2,128)S(1)}, f32[2,256]{1,0:T(2,128)S(1)}, u32[]{:S(2)}, u32[]{:S(2)}) collective-permute-start(f32[2,256]{1,0:T(2,128)S(1)} %pad_maximum_fusion.1), channel_id=1, source_target_pairs={{0,4},{4,0},{8,12},{12,8},{1,5},{5,1},{9,13},{13,9},{2,6},{6,2},{1... | collective-permute-start | bytes 6152 | tf_op jit(solution)/shard_map/ppermute | solution.py:101
  89.9 21.4 %collective-permute-start = (f32[2,256]{1,0:T(2,128)S(1)}, f32[2,256]{1,0:T(2,128)S(1)}, u32[]{:S(2)}, u32[]{:S(2)}) collective-permute-start(f32[2,256]{1,0:T(2,128)S(1)} %pad_maximum_fusion), channel_id=1, source_target_pairs={{0,4},{4,0},{8,12},{12,8},{1,5},{5,1},{9,13},{13,9},{2,6},{6,2},{1... | collective-permute-start | bytes 6152 | tf_op jit(solution)/shard_map/ppermute | solution.py:101
  109.1 19.8 %collective-permute-start.13 = (f32[2,256]{1,0:T(2,128)S(1)}, f32[2,256]{1,0:T(2,128)S(1)}, u32[]{:S(2)}, u32[]{:S(2)}) collective-permute-start(f32[2,256]{1,0:T(2,128)S(1)} %fusion.196), channel_id=1, source_target_pairs={{0,8},{4,12},{8,0},{12,4},{1,9},{5,13},{9,1},{13,5},{2,10},{6,14},... | collective-permute-start | bytes 6152 | tf_op jit(solution)/shard_map/ppermute | solution.py:101
  109.7 40.0 %collective-permute-start.7 = (f32[2,256]{1,0:T(2,128)S(1)}, f32[2,256]{1,0:T(2,128)S(1)}, u32[]{:S(2)}, u32[]{:S(2)}) collective-permute-start(f32[2,256]{1,0:T(2,128)S(1)} %fusion.197), channel_id=1, source_target_pairs={{0,8},{4,12},{8,0},{12,4},{1,9},{5,13},{9,1},{13,5},{2,10},{6,14},... | collective-permute-start | bytes 6152 | tf_op jit(solution)/shard_map/ppermute | solution.py:101
  111.3 58.8 %collective-permute-start.1 = (f32[2,256]{1,0:T(2,128)S(1)}, f32[2,256]{1,0:T(2,128)S(1)}, u32[]{:S(2)}, u32[]{:S(2)}) collective-permute-start(f32[2,256]{1,0:T(2,128)S(1)} %fusion.198), channel_id=1, source_target_pairs={{0,8},{4,12},{8,0},{12,4},{1,9},{5,13},{9,1},{13,5},{2,10},{6,14},... | collective-permute-start | bytes 6152 | tf_op jit(solution)/shard_map/ppermute | solution.py:101
  128.9 71.2 %collective-permute-start.20 = (bf16[2,3,256,256]{3,2,1,0:T(8,128)(2,1)}, bf16[2,3,256,256]{3,2,1,0:T(8,128)(2,1)}, u32[]{:S(2)}, u32[]{:S(2)}) collective-permute-start(bf16[2,3,256,256]{3,2,1,0:T(8,128)(2,1)} %bitcast.463), channel_id=1, source_target_pairs={{0,4},{4,0},{8,12},{12,8},{1,5},{5,1},{9,13},{13,9},{2,6},{6,2},{1... | collective-permute-start | bytes 2359304 | tf_op jit(solution)/shard_map/ppermute | solution.py:101
  149.4 53.3 %collective-permute-start.14 = (bf16[2,3,256,256]{3,2,1,0:T(8,128)(2,1)}, bf16[2,3,256,256]{3,2,1,0:T(8,128)(2,1)}, u32[]{:S(2)}, u32[]{:S(2)}) collective-permute-start(bf16[2,3,256,256]{3,2,1,0:T(8,128)(2,1)} %bitcast.464), channel_id=1, source_target_pairs={{0,4},{4,0},{8,12},{12,8},{1,5},{5,1},{9,13},{13,9},{2,6},{6,2},{1... | collective-permute-start | bytes 2359304 | tf_op jit(solution)/shard_map/ppermute | solution.py:101
  169.9 35.2 %collective-permute-start.8 = (bf16[2,3,256,256]{3,2,1,0:T(8,128)(2,1)}, bf16[2,3,256,256]{3,2,1,0:T(8,128)(2,1)}, u32[]{:S(2)}, u32[]{:S(2)}) collective-permute-start(bf16[2,3,256,256]{3,2,1,0:T(8,128)(2,1)} %bitcast.465), channel_id=1, source_target_pairs={{0,4},{4,0},{8,12},{12,8},{1,5},{5,1},{9,13},{13,9},{2,6},{6,2},{1... | collective-permute-start | bytes 2359304 | tf_op jit(solution)/shard_map/ppermute | solution.py:101
  189.6 18.8 %collective-permute-start.2 = (bf16[2,3,256,256]{3,2,1,0:T(8,128)(2,1)S(1)}, bf16[2,3,256,256]{3,2,1,0:T(8,128)(2,1)S(1)}, u32[]{:S(2)}, u32[]{:S(2)}) collective-permute-start(bf16[2,3,256,256]{3,2,1,0:T(8,128)(2,1)S(1)} %bitcast.525), channel_id=1, source_target_pairs={{0,4},{4,0},{8,12},{12,8},{1,5},{5,1},{9,13},{13,9},{2,6},{6,2},{1... | collective-permute-start | bytes 2359304 | tf_op jit(solution)/shard_map/ppermute | solution.py:101
  201.1 12.0 %collective-permute-start.21 = (bf16[3,256,256]{2,1,0:T(8,128)(2,1)S(1)}, bf16[3,256,256]{2,1,0:T(8,128)(2,1)S(1)}, u32[]{:S(2)}, u32[]{:S(2)}) collective-permute-start(bf16[3,256,256]{2,1,0:T(8,128)(2,1)S(1)} %fusion.125), channel_id=1, source_target_pairs={{0,8},{4,12},{8,0},{12,4},{1,9},{5,13},{9,1},{13,5},{2,10},{6,14},... | collective-permute-start | bytes 1179656 | tf_op jit(solution)/shard_map/ppermute | solution.py:101
  204.5 20.4 %collective-permute-start.15 = (bf16[3,256,256]{2,1,0:T(8,128)(2,1)}, bf16[3,256,256]{2,1,0:T(8,128)(2,1)}, u32[]{:S(2)}, u32[]{:S(2)}) collective-permute-start(bf16[3,256,256]{2,1,0:T(8,128)(2,1)} %fusion.128), channel_id=1, source_target_pairs={{0,8},{4,12},{8,0},{12,4},{1,9},{5,13},{9,1},{13,5},{2,10},{6,14},... | collective-permute-start | bytes 1179656 | tf_op jit(solution)/shard_map/ppermute | solution.py:101
  206.9 53.3 %collective-permute-start.9 = (bf16[3,256,256]{2,1,0:T(8,128)(2,1)}, bf16[3,256,256]{2,1,0:T(8,128)(2,1)}, u32[]{:S(2)}, u32[]{:S(2)}) collective-permute-start(bf16[3,256,256]{2,1,0:T(8,128)(2,1)} %fusion.131), channel_id=1, source_target_pairs={{0,8},{4,12},{8,0},{12,4},{1,9},{5,13},{9,1},{13,5},{2,10},{6,14},... | collective-permute-start | bytes 1179656 | tf_op jit(solution)/shard_map/ppermute | solution.py:101
  209.4 73.8 %collective-permute-start.3 = (bf16[3,256,256]{2,1,0:T(8,128)(2,1)}, bf16[3,256,256]{2,1,0:T(8,128)(2,1)}, u32[]{:S(2)}, u32[]{:S(2)}) collective-permute-start(bf16[3,256,256]{2,1,0:T(8,128)(2,1)} %fusion.134), channel_id=1, source_target_pairs={{0,8},{4,12},{8,0},{12,4},{1,9},{5,13},{9,1},{13,5},{2,10},{6,14},... | collective-permute-start | bytes 1179656 | tf_op jit(solution)/shard_map/ppermute | solution.py:101
  222.6 18.0 %collective-permute-start.22 = (bf16[256,256]{1,0:T(8,128)(2,1)}, bf16[256,256]{1,0:T(8,128)(2,1)S(1)}, u32[]{:S(2)}, u32[]{:S(2)}) collective-permute-start(bf16[256,256]{1,0:T(8,128)(2,1)} %copy.101), channel_id=1, source_target_pairs={{0,8},{4,12},{8,0},{12,4},{1,9},{5,13},{9,1},{13,5},{2,10},{6,14},... | collective-permute-start | bytes 393224 | tf_op jit(solution)/shard_map/ppermute | solution.py:101
  252.9 64.6 %reduce-scatter.10.cloned.1.call-start = ((), (), s32[]{:S(2)}) async-start(), calls=%async_computation.7 | async-start | bytes 983040 | tf_op jit(solution)/shard_map/reduce_scatter | solution.py:178
  275.8 50.1 %reduce-scatter.8.cloned.1.call-start = ((), (), s32[]{:S(2)}) async-start(), calls=%async_computation.6 | async-start | bytes 983040 | tf_op jit(solution)/shard_map/reduce_scatter | solution.py:178
  280.9 6.1 %collective-permute-start.10 = (bf16[256,256]{1,0:T(8,128)(2,1)}, bf16[256,256]{1,0:T(8,128)(2,1)S(1)}, u32[]{:S(2)}, u32[]{:S(2)}) collective-permute-start(bf16[256,256]{1,0:T(8,128)(2,1)} %copy.65), channel_id=1, source_target_pairs={{0,8},{4,12},{8,0},{12,4},{1,9},{5,13},{9,1},{13,5},{2,10},{6,14},... | collective-permute-start | bytes 393224 | tf_op jit(solution)/shard_map/ppermute | solution.py:101
  299.8 50.9 %reduce-scatter.6.cloned.1.call-start = ((), (), s32[]{:S(2)}) async-start(), calls=%async_computation.5 | async-start | bytes 983040 | tf_op jit(solution)/shard_map/reduce_scatter | solution.py:178
  317.4 228.7 %reduce-scatter.14.cloned.1.call-start = ((), (), s32[]{:S(2)}) async-start(), calls=%async_computation.9 | async-start | bytes 983040 | tf_op jit(solution)/shard_map/reduce_scatter | solution.py:198
  361.8 9.7 %collective-permute-start.53 = (bf16[64,1536]{1,0:T(8,128)(2,1)S(1)}, bf16[64,1536]{1,0:T(8,128)(2,1)S(1)}, u32[]{:S(2)}, u32[]{:S(2)}) collective-permute-start(bf16[64,1536]{1,0:T(8,128)(2,1)S(1)} %get-tuple-element.55), channel_id=1, source_target_pairs={{0,1},{1,2},{2,3},{3,0},{4,5},{5,6},{6,7},{7,4},{8,9},{9,10},{10,1... | collective-permute-start | bytes 589832 | tf_op jit(solution)/shard_map/ppermute | solution.py:183
  362.2 13.4 %collective-permute-start.44 = (bf16[64,1536]{1,0:T(8,128)(2,1)S(1)}, bf16[64,1536]{1,0:T(8,128)(2,1)S(1)}, u32[]{:S(2)}, u32[]{:S(2)}) collective-permute-start(bf16[64,1536]{1,0:T(8,128)(2,1)S(1)} %get-tuple-element.53), channel_id=1, source_target_pairs={{0,1},{1,2},{2,3},{3,0},{4,5},{5,6},{6,7},{7,4},{8,9},{9,10},{10,1... | collective-permute-start | bytes 589832 | tf_op jit(solution)/shard_map/ppermute | solution.py:183
  363.6 16.3 %collective-permute-start.35 = (bf16[64,1536]{1,0:T(8,128)(2,1)S(1)}, bf16[64,1536]{1,0:T(8,128)(2,1)S(1)}, u32[]{:S(2)}, u32[]{:S(2)}) collective-permute-start(bf16[64,1536]{1,0:T(8,128)(2,1)S(1)} %get-tuple-element.54), channel_id=1, source_target_pairs={{0,1},{1,2},{2,3},{3,0},{4,5},{5,6},{6,7},{7,4},{8,9},{9,10},{10,1... | collective-permute-start | bytes 589832 | tf_op jit(solution)/shard_map/ppermute | solution.py:183
  365.1 19.0 %collective-permute-start.26 = (bf16[64,1536]{1,0:T(8,128)(2,1)S(1)}, bf16[64,1536]{1,0:T(8,128)(2,1)S(1)}, u32[]{:S(2)}, u32[]{:S(2)}) collective-permute-start(bf16[64,1536]{1,0:T(8,128)(2,1)S(1)} %get-tuple-element.52), channel_id=1, source_target_pairs={{0,1},{1,2},{2,3},{3,0},{4,5},{5,6},{6,7},{7,4},{8,9},{9,10},{10,1... | collective-permute-start | bytes 589832 | tf_op jit(solution)/shard_map/ppermute | solution.py:183
  371.5 16.9 %collective-permute-start.54 = (bf16[64,1536]{1,0:T(8,128)(2,1)S(1)}, bf16[64,1536]{1,0:T(8,128)(2,1)S(1)}, u32[]{:S(2)}, u32[]{:S(2)}) collective-permute-start(bf16[64,1536]{1,0:T(8,128)(2,1)S(1)} %collective-permute-done.53), channel_id=1, source_target_pairs={{0,1},{1,2},{2,3},{3,0},{4,5},{5,6},{6,7},{7,4},{8,9},{9,10},{10,1... | collective-permute-start | bytes 589832 | tf_op jit(solution)/shard_map/ppermute | solution.py:183
  375.7 17.0 %collective-permute-start.45 = (bf16[64,1536]{1,0:T(8,128)(2,1)S(1)}, bf16[64,1536]{1,0:T(8,128)(2,1)}, u32[]{:S(2)}, u32[]{:S(2)}) collective-permute-start(bf16[64,1536]{1,0:T(8,128)(2,1)S(1)} %collective-permute-done.44), channel_id=1, source_target_pairs={{0,1},{1,2},{2,3},{3,0},{4,5},{5,6},{6,7},{7,4},{8,9},{9,10},{10,1... | collective-permute-start | bytes 589832 | tf_op jit(solution)/shard_map/ppermute | solution.py:183
  379.9 17.0 %collective-permute-start.36 = (bf16[64,1536]{1,0:T(8,128)(2,1)S(1)}, bf16[64,1536]{1,0:T(8,128)(2,1)}, u32[]{:S(2)}, u32[]{:S(2)}) collective-permute-start(bf16[64,1536]{1,0:T(8,128)(2,1)S(1)} %collective-permute-done.35), channel_id=1, source_target_pairs={{0,1},{1,2},{2,3},{3,0},{4,5},{5,6},{6,7},{7,4},{8,9},{9,10},{10,1... | collective-permute-start | bytes 589832 | tf_op jit(solution)/shard_map/ppermute | solution.py:183
  384.1 17.0 %collective-permute-start.27 = (bf16[64,1536]{1,0:T(8,128)(2,1)S(1)}, bf16[64,1536]{1,0:T(8,128)(2,1)}, u32[]{:S(2)}, u32[]{:S(2)}) collective-permute-start(bf16[64,1536]{1,0:T(8,128)(2,1)S(1)} %collective-permute-done.26), channel_id=1, source_target_pairs={{0,1},{1,2},{2,3},{3,0},{4,5},{5,6},{6,7},{7,4},{8,9},{9,10},{10,1... | collective-permute-start | bytes 589832 | tf_op jit(solution)/shard_map/ppermute | solution.py:183
  388.3 16.9 %collective-permute-start.55 = (bf16[64,1536]{1,0:T(8,128)(2,1)S(1)}, bf16[64,1536]{1,0:T(8,128)(2,1)S(1)}, u32[]{:S(2)}, u32[]{:S(2)}) collective-permute-start(bf16[64,1536]{1,0:T(8,128)(2,1)S(1)} %collective-permute-done.54), channel_id=1, source_target_pairs={{0,1},{1,2},{2,3},{3,0},{4,5},{5,6},{6,7},{7,4},{8,9},{9,10},{10,1... | collective-permute-start | bytes 589832 | tf_op jit(solution)/shard_map/ppermute | solution.py:183
  392.6 20.6 %collective-permute-start.46 = (bf16[64,1536]{1,0:T(8,128)(2,1)}, bf16[64,1536]{1,0:T(8,128)(2,1)S(1)}, u32[]{:S(2)}, u32[]{:S(2)}) collective-permute-start(bf16[64,1536]{1,0:T(8,128)(2,1)} %collective-permute-done.45), channel_id=1, source_target_pairs={{0,1},{1,2},{2,3},{3,0},{4,5},{5,6},{6,7},{7,4},{8,9},{9,10},{10,1... | collective-permute-start | bytes 589832 | tf_op jit(solution)/shard_map/ppermute | solution.py:183
  396.9 25.1 %collective-permute-start.37 = (bf16[64,1536]{1,0:T(8,128)(2,1)}, bf16[64,1536]{1,0:T(8,128)(2,1)S(1)}, u32[]{:S(2)}, u32[]{:S(2)}) collective-permute-start(bf16[64,1536]{1,0:T(8,128)(2,1)} %collective-permute-done.36), channel_id=1, source_target_pairs={{0,1},{1,2},{2,3},{3,0},{4,5},{5,6},{6,7},{7,4},{8,9},{9,10},{10,1... | collective-permute-start | bytes 589832 | tf_op jit(solution)/shard_map/ppermute | solution.py:183
  401.1 26.9 %collective-permute-start.28 = (bf16[64,1536]{1,0:T(8,128)(2,1)}, bf16[64,1536]{1,0:T(8,128)(2,1)S(1)}, u32[]{:S(2)}, u32[]{:S(2)}) collective-permute-start(bf16[64,1536]{1,0:T(8,128)(2,1)} %collective-permute-done.27), channel_id=1, source_target_pairs={{0,1},{1,2},{2,3},{3,0},{4,5},{5,6},{6,7},{7,4},{8,9},{9,10},{10,1... | collective-permute-start | bytes 589832 | tf_op jit(solution)/shard_map/ppermute | solution.py:183
  413.1 21.0 %collective-permute-start.56 = (bf16[2,64,3072]{2,1,0:T(8,128)(2,1)S(1)}, bf16[2,64,3072]{2,1,0:T(8,128)(2,1)S(1)}, u32[]{:S(2)}, u32[]{:S(2)}) collective-permute-start(bf16[2,64,3072]{2,1,0:T(8,128)(2,1)S(1)} %dynamic-slice_bitcast_fusion), channel_id=1, source_target_pairs={{0,4},{4,0},{8,12},{12,8},{1,5},{5,1},{9,13},{13,9},{2,6},{6,2},{1... | collective-permute-start | bytes 2359304 | tf_op jit(solution)/shard_map/ppermute | solution.py:101
  421.9 13.0 %collective-permute-start.47 = (bf16[2,64,3072]{2,1,0:T(8,128)(2,1)S(1)}, bf16[2,64,3072]{2,1,0:T(8,128)(2,1)S(1)}, u32[]{:S(2)}, u32[]{:S(2)}) collective-permute-start(bf16[2,64,3072]{2,1,0:T(8,128)(2,1)S(1)} %dynamic-slice_bitcast_fusion.1), channel_id=1, source_target_pairs={{0,4},{4,0},{8,12},{12,8},{1,5},{5,1},{9,13},{13,9},{2,6},{6,2},{1... | collective-permute-start | bytes 2359304 | tf_op jit(solution)/shard_map/ppermute | solution.py:101
  427.9 8.6 %collective-permute-start.38 = (bf16[2,64,3072]{2,1,0:T(8,128)(2,1)S(1)}, bf16[2,64,3072]{2,1,0:T(8,128)(2,1)S(1)}, u32[]{:S(2)}, u32[]{:S(2)}) collective-permute-start(bf16[2,64,3072]{2,1,0:T(8,128)(2,1)S(1)} %dynamic-slice_bitcast_fusion.2), channel_id=1, source_target_pairs={{0,4},{4,0},{8,12},{12,8},{1,5},{5,1},{9,13},{13,9},{2,6},{6,2},{1... | collective-permute-start | bytes 2359304 | tf_op jit(solution)/shard_map/ppermute | solution.py:101
  434.2 12.0 %collective-permute-start.57 = (bf16[64,3072]{1,0:T(8,128)(2,1)S(1)}, bf16[64,3072]{1,0:T(8,128)(2,1)S(1)}, u32[]{:S(2)}, u32[]{:S(2)}) collective-permute-start(bf16[64,3072]{1,0:T(8,128)(2,1)S(1)} %fusion.113), channel_id=1, source_target_pairs={{0,8},{4,12},{8,0},{12,4},{1,9},{5,13},{9,1},{13,5},{2,10},{6,14},... | collective-permute-start | bytes 1179656 | tf_op jit(solution)/shard_map/ppermute | solution.py:101
  435.0 19.7 %collective-permute-start.48 = (bf16[64,3072]{1,0:T(8,128)(2,1)S(1)}, bf16[64,3072]{1,0:T(8,128)(2,1)S(1)}, u32[]{:S(2)}, u32[]{:S(2)}) collective-permute-start(bf16[64,3072]{1,0:T(8,128)(2,1)S(1)} %fusion.116), channel_id=1, source_target_pairs={{0,8},{4,12},{8,0},{12,4},{1,9},{5,13},{9,1},{13,5},{2,10},{6,14},... | collective-permute-start | bytes 1179656 | tf_op jit(solution)/shard_map/ppermute | solution.py:101
  436.6 26.5 %collective-permute-start.39 = (bf16[64,3072]{1,0:T(8,128)(2,1)S(1)}, bf16[64,3072]{1,0:T(8,128)(2,1)S(1)}, u32[]{:S(2)}, u32[]{:S(2)}) collective-permute-start(bf16[64,3072]{1,0:T(8,128)(2,1)S(1)} %fusion.119), channel_id=1, source_target_pairs={{0,8},{4,12},{8,0},{12,4},{1,9},{5,13},{9,1},{13,5},{2,10},{6,14},... | collective-permute-start | bytes 1179656 | tf_op jit(solution)/shard_map/ppermute | solution.py:101
  437.3 33.8 %collective-permute-start.30 = (bf16[64,3072]{1,0:T(8,128)(2,1)S(1)}, bf16[64,3072]{1,0:T(8,128)(2,1)S(1)}, u32[]{:S(2)}, u32[]{:S(2)}) collective-permute-start(bf16[64,3072]{1,0:T(8,128)(2,1)S(1)} %fusion.122), channel_id=1, source_target_pairs={{0,8},{4,12},{8,0},{12,4},{1,9},{5,13},{9,1},{13,5},{2,10},{6,14},... | collective-permute-start | bytes 1179656 | tf_op jit(solution)/shard_map/ppermute | solution.py:101
  472.7 12.1 %collective-permute-start.31 = (bf16[64,3072]{1,0:T(8,128)(2,1)S(1)}, bf16[64,3072]{1,0:T(8,128)(2,1)S(1)}, u32[]{:S(2)}, u32[]{:S(2)}) collective-permute-start(bf16[64,3072]{1,0:T(8,128)(2,1)S(1)} %get-tuple-element.72), channel_id=1, source_target_pairs={{0,8},{4,12},{8,0},{12,4},{1,9},{5,13},{9,1},{13,5},{2,10},{6,14},... | collective-permute-start | bytes 1179656 | tf_op jit(solution)/shard_map/ppermute | solution.py:101
  473.3 19.9 %collective-permute-start.40 = (bf16[64,3072]{1,0:T(8,128)(2,1)S(1)}, bf16[64,3072]{1,0:T(8,128)(2,1)S(1)}, u32[]{:S(2)}, u32[]{:S(2)}) collective-permute-start(bf16[64,3072]{1,0:T(8,128)(2,1)S(1)} %get-tuple-element.73), channel_id=1, source_target_pairs={{0,8},{4,12},{8,0},{12,4},{1,9},{5,13},{9,1},{13,5},{2,10},{6,14},... | collective-permute-start | bytes 1179656 | tf_op jit(solution)/shard_map/ppermute | solution.py:101
  474.8 26.9 %collective-permute-start.49 = (bf16[64,3072]{1,0:T(8,128)(2,1)S(1)}, bf16[64,3072]{1,0:T(8,128)(2,1)S(1)}, u32[]{:S(2)}, u32[]{:S(2)}) collective-permute-start(bf16[64,3072]{1,0:T(8,128)(2,1)S(1)} %get-tuple-element.74), channel_id=1, source_target_pairs={{0,8},{4,12},{8,0},{12,4},{1,9},{5,13},{9,1},{13,5},{2,10},{6,14},... | collective-permute-start | bytes 1179656 | tf_op jit(solution)/shard_map/ppermute | solution.py:101
  475.4 33.4 %collective-permute-start.58 = (bf16[64,3072]{1,0:T(8,128)(2,1)S(1)}, bf16[64,3072]{1,0:T(8,128)(2,1)S(1)}, u32[]{:S(2)}, u32[]{:S(2)}) collective-permute-start(bf16[64,3072]{1,0:T(8,128)(2,1)S(1)} %get-tuple-element.75), channel_id=1, source_target_pairs={{0,8},{4,12},{8,0},{12,4},{1,9},{5,13},{9,1},{13,5},{2,10},{6,14},... | collective-permute-start | bytes 1179656 | tf_op jit(solution)/shard_map/ppermute | solution.py:101
  484.9 26.7 %collective-permute-start.32 = (bf16[2,64,3072]{2,1,0:T(8,128)(2,1)S(1)}, bf16[2,64,3072]{2,1,0:T(8,128)(2,1)S(1)}, u32[]{:S(2)}, u32[]{:S(2)}) collective-permute-start(bf16[2,64,3072]{2,1,0:T(8,128)(2,1)S(1)} %maximum_select_fusion.4), channel_id=1, source_target_pairs={{0,4},{4,0},{8,12},{12,8},{1,5},{5,1},{9,13},{13,9},{2,6},{6,2},{1... | collective-permute-start | bytes 2359304 | tf_op jit(solution)/shard_map/ppermute | solution.py:101
  493.4 16.2 %collective-permute-start.41 = (bf16[2,64,3072]{2,1,0:T(8,128)(2,1)S(1)}, bf16[2,64,3072]{2,1,0:T(8,128)(2,1)S(1)}, u32[]{:S(2)}, u32[]{:S(2)}) collective-permute-start(bf16[2,64,3072]{2,1,0:T(8,128)(2,1)S(1)} %maximum_select_fusion.6), channel_id=1, source_target_pairs={{0,4},{4,0},{8,12},{12,8},{1,5},{5,1},{9,13},{13,9},{2,6},{6,2},{1... | collective-permute-start | bytes 2359304 | tf_op jit(solution)/shard_map/ppermute | solution.py:101
  501.8 8.2 %collective-permute-start.50 = (bf16[2,64,3072]{2,1,0:T(8,128)(2,1)S(1)}, bf16[2,64,3072]{2,1,0:T(8,128)(2,1)S(1)}, u32[]{:S(2)}, u32[]{:S(2)}) collective-permute-start(bf16[2,64,3072]{2,1,0:T(8,128)(2,1)S(1)} %maximum_select_fusion.7), channel_id=1, source_target_pairs={{0,4},{4,0},{8,12},{12,8},{1,5},{5,1},{9,13},{13,9},{2,6},{6,2},{1... | collective-permute-start | bytes 2359304 | tf_op jit(solution)/shard_map/ppermute | solution.py:101
  (82 other events, 1467.8 us)
Sparse Core Ops, SparseCore 0:
  253.0 23.1 reduce-scatter.11
  278.4 22.5 reduce-scatter.9
  303.3 22.5 reduce-scatter.7
  328.1 22.5 reduce-scatter.5
  525.4 20.7 reduce-scatter.13
